TPU v7x, 128 devices: a whole 4x4x4 slice. The times are simulated.
128 devices in a mesh: ctx: 32 (over y, z, core), fsdp: 4 (over x).
Axes of the slice: x: 4, y: 4, z: 4, core: 2. Of those that a mesh axis runs over, the one named last changes fastest.
Arguments:
- gate_in: bfloat16 [16384, 4096], P('ctx', 'fsdp'), may hold values from -6 to 6
- values: bfloat16 [16384, 4096], P('ctx', 'fsdp'), may hold values from -6 to 6
- gate_out: bfloat16 [16384, 4096], P('ctx', 'fsdp'), may hold values from -6 to 6
- bias: float32 [4096], P('fsdp'), may hold values from -4 to 4
- spectrum: bfloat16 [2, 32768, 4096], P(None, ('ctx', 'fsdp')), may hold values from -6 to 6
Outputs:
- gated: bfloat16 [16384, 4096], P('ctx', 'fsdp')
All inputs are finite; a program needn't handle non-finite values.
Results may differ from a plain program's by a relative error of at most 0.0049.
Values may be sent and summed in bfloat16 or wider, within the bound.
No kernel may reach another device: no remote copies, remote signals or barrier semaphores. Data moves between devices by JAX's collectives and lax.ppermute only.
A program may use at most 128 MiB of HBM per device.

v0:
```python
import math
import jax
import jax.numpy as jnp
from jax import lax
from jax.sharding import PartitionSpec as P


def phase_angles(rows_side, cols_side, modulus):
    product = rows_side[:, None] * cols_side[None, :] % modulus
    return product.astype(jnp.float32) * (2.0 * math.pi / modulus)


def contract(matrix, operand):
    return jnp.einsum("kj,sjc->skc", matrix, operand, precision=lax.Precision.HIGHEST)


def mix_rows(matrix, operand):
    return jnp.einsum("kp,pjc->kjc", matrix, operand, precision=lax.Precision.HIGHEST)


def body(gate_in, values, gate_out, bias, spectrum):
    devices = lax.axis_size("ctx")
    rows_here = gate_in.shape[0]
    channels = gate_in.shape[1]
    block_rows = rows_here // devices
    length_total = 2 * rows_here * devices
    position = lax.axis_index("ctx")
    mixed = (gate_in.astype(jnp.float32) * values.astype(jnp.float32)).astype(jnp.bfloat16)
    mixed = lax.optimization_barrier(mixed)
    member = lax.axis_index("fsdp")
    filter_here = lax.dynamic_slice_in_dim(
        lax.all_gather(spectrum, "fsdp", axis=1, tiled=True), member * channels, channels, 2
    )
    source_index = jnp.arange(devices, dtype=jnp.int32)
    mirror_index = jnp.where(source_index == 0, devices, 2 * devices - source_index)
    radix_order = jnp.stack([source_index, mirror_index], axis=1).reshape(2 * devices)
    cross_angle = phase_angles(radix_order, source_index, 2 * devices)
    cross_cos = jnp.cos(cross_angle)
    cross_sin = jnp.sin(cross_angle)
    local_rows = position * block_rows + jnp.arange(block_rows, dtype=jnp.int32)
    twist_angle = (radix_order[:, None] * local_rows[None, :] % length_total).astype(
        jnp.float32
    ) * (2.0 * math.pi / length_total)
    twist_cos = jnp.cos(twist_angle)[:, :, None]
    twist_sin = jnp.sin(twist_angle)[:, :, None]
    source = mixed[None]
    width_now = source.shape[2]
    real_in = lax.all_to_all(
        source.reshape(source.shape[0], devices, block_rows, width_now),
        "ctx",
        split_axis=1,
        concat_axis=1,
        tiled=True,
    )[0].astype(jnp.float32)
    real_mix = mix_rows(cross_cos, real_in)
    imag_mix = -mix_rows(cross_sin, real_in)
    spread = jnp.stack(
        [real_mix * twist_cos + imag_mix * twist_sin, imag_mix * twist_cos - real_mix * twist_sin]
    )
    regrouped = lax.all_to_all(spread, "ctx", split_axis=1, concat_axis=2, tiled=True)
    row_index = jnp.arange(rows_here, dtype=jnp.int32)
    local_angle = phase_angles(row_index, row_index, rows_here)
    local_cos = jnp.cos(local_angle)
    local_sin = jnp.sin(local_angle)
    real_part = regrouped[0]
    imag_part = regrouped[1]
    freq_real = contract(local_cos, real_part) + contract(local_sin, imag_part)
    freq_imag = contract(local_cos, imag_part) - contract(local_sin, real_part)
    filter_float = filter_here.astype(jnp.float32).reshape(2, 2, rows_here, channels)
    prod_real = freq_real * filter_float[0] - freq_imag * filter_float[1]
    prod_imag = freq_real * filter_float[1] + freq_imag * filter_float[0]
    back_real = contract(local_cos, prod_real) - contract(local_sin, prod_imag)
    back_imag = contract(local_cos, prod_imag) + contract(local_sin, prod_real)
    pair_index = jnp.stack([position, jnp.where(position == 0, devices, 2 * devices - position)])
    back_angle = (pair_index[:, None] * row_index[None, :] % length_total).astype(jnp.float32) * (
        2.0 * math.pi / length_total
    )
    back_cos = jnp.cos(back_angle)[:, :, None]
    back_sin = jnp.sin(back_angle)[:, :, None]
    turned_real = back_real * back_cos - back_imag * back_sin
    turned_imag = back_real * back_sin + back_imag * back_cos
    stacked = jnp.stack([turned_real, turned_imag]).reshape(2, 2, devices, block_rows, width_now)
    inverse_angle = phase_angles(source_index, radix_order, 2 * devices)
    inverse_cos = jnp.cos(inverse_angle) / length_total
    inverse_sin = jnp.sin(inverse_angle) / length_total
    received = lax.all_to_all(stacked, "ctx", split_axis=2, concat_axis=1, tiled=True)
    real_block = received[0, :, 0]
    imag_block = received[1, :, 0]
    real_out = mix_rows(inverse_cos, real_block) - mix_rows(inverse_sin, imag_block)
    folded = real_out[None]
    restored = lax.all_to_all(folded, "ctx", split_axis=1, concat_axis=1, tiled=True)
    restored = restored.reshape(restored.shape[0], rows_here, width_now)
    convolved_part = restored[0]
    convolved = convolved_part + bias[None, :] * mixed.astype(jnp.float32)
    return (gate_out.astype(jnp.float32) * convolved).astype(jnp.bfloat16)


def solution(mesh):
    return jax.shard_map(
        body,
        mesh=mesh,
        in_specs=(
            P("ctx", "fsdp"),
            P("ctx", "fsdp"),
            P("ctx", "fsdp"),
            P("fsdp"),
            P(None, ("ctx", "fsdp"), None),
        ),
        out_specs=P("ctx", "fsdp"),
        check_vma=False,
    )
```

profile of v0, /device:TPU:1, one launch (start us, length us, event | category | flops | bytes accessed | tf_op | source)
XLA Modules:
  0.0 493.6 jit_solution(11693524858831694724)
XLA Ops:
  9.4 9.6 %all-to-all-start = ((bf16[1,32,16,1024]{3,2,0,1:T(8,128)(2,1)}), bf16[1,32,16,1024]{3,2,0,1:T(8,128)(2,1)S(1)}, u32[]{:S(2)}, u32[]{:S(2)}) async-start(bf16[1,32,16,1024]{3,2,0,1:T(8,128)(2,1)} %bitcast.3), calls=%async_computation | async-start | bytes 2097152 | tf_op jit(solution)/shard_map/all_to_all | solution.py:48
  19.4 16.5 %all-to-all-done = bf16[1,32,16,1024]{3,2,0,1:T(8,128)(2,1)S(1)} async-done(((bf16[1,32,16,1024]{3,2,0,1:T(8,128)(2,1)}), bf16[1,32,16,1024]{3,2,0,1:T(8,128)(2,1)S(1)}, u32[]{:S(2)}, u32[]{:S(2)}) %all-to-all-start) | async-done | bytes 1048608 | tf_op jit(solution)/shard_map/all_to_all | solution.py:48
  38.6 3.6 add_bitcast_fusion
  43.9 8.3 %copy.55 = f32[2,64,16,1024]{3,2,0,1:T(8,128)} copy(f32[2,64,16,1024]{3,1,2,0:T(8,128)S(1)} %pad_maximum_fusion) | data formatting | bytes 16777216 | tf_op jit(solution)/shard_map/stack | solution.py:57
  52.1 4.8 all-to-all-start.1
  57.2 104.1 %all-to-all-done.1 = f32[2,64,16,1024]{3,2,0,1:T(8,128)} async-done(((f32[2,64,16,1024]{3,2,0,1:T(8,128)}), f32[2,64,16,1024]{3,2,0,1:T(8,128)}, u32[]{:S(2)}, u32[]{:S(2)}) %all-to-all-start.1) | async-done | bytes 8388640 | tf_op jit(solution)/shard_map/all_to_all | solution.py:60
  161.3 4.2 copy.56
  169.7 17.0 %fusion.23 = f32[2,1024,512]{2,1,0:T(8,128)S(1)} fusion(f32[2,512,1024]{2,1,0:T(8,128)S(1)} %bitcast.102), kind=kOutput, calls=%fused_computation.42 | convolution fusion | flops 6446120960 | bytes 8388608 | tf_op jit(solution)/shard_map/kj,sjc->skc/dot_general | solution.py:14
  186.7 18.7 %fusion.21 = f32[2,1024,512]{2,1,0:T(8,128)} fusion(f32[2,512,1024]{2,1,0:T(8,128)S(1)} %bitcast.100), kind=kOutput, calls=%fused_computation.40 | convolution fusion | flops 6446120960 | bytes 8388608 | tf_op jit(solution)/shard_map/kj,sjc->skc/dot_general | solution.py:14
  205.4 18.5 %convolution_add_fusion.1 = f32[2,1024,512]{2,1,0:T(8,128)} fusion(f32[2,1024,512]{2,1,0:T(8,128)S(1)} %fusion.23, f32[2,512,1024]{2,1,0:T(8,128)S(1)} %bitcast.101), kind=kOutput, calls=%fused_computation.20 | convolution fusion | flops 6447169536 | bytes 12582912 | tf_op jit(solution)/shard_map/kj,sjc->skc/dot_general | solution.py:14
  223.9 3.2 dynamic-slice_convert_fusion
  227.1 4.1 fusion.133
  231.2 5.4 %copy.64 = f32[2,512,1024]{1,2,0:T(8,128)} copy(f32[2,512,1024]{2,1,0:T(8,128)} %bitcast.108) | data formatting | bytes 8388608 | tf_op jit(solution)/shard_map/squeeze | solution.py:70
  236.6 5.4 %copy.61 = f32[2,512,1024]{1,2,0:T(8,128)} copy(f32[2,512,1024]{2,1,0:T(8,128)} %bitcast.107) | data formatting | bytes 8388608 | tf_op jit(solution)/shard_map/squeeze | solution.py:70
  242.1 26.0 %fusion.4 = (f32[2,512,1024]{1,2,0:T(8,128)S(1)}, f32[2,512,1024]{1,2,0:T(8,128)S(1)}) fusion(f32[2,512,1024]{1,2,0:T(8,128)} %copy.64, f32[2,512,1024]{1,2,0:T(8,128)} %copy.61, f32[2,1024,512]{2,1,0:T(8,128)} %convolution_add_fusion.1, f32[2,1024,512]{2,1,0:T(8,128)} %fusion.21, f32[2,512,1024]{2,1,0:T(8,128)} %bitcast.103), kind=kOutput, calls=%fused_computation.8 | convolution fusion | flops 6453460992 | bytes 29360128 | tf_op jit(solution)/shard_map/kj,sjc->skc/dot_general | solution.py:14
  268.0 10.7 %fusion.19 = f32[2,1024,512]{1,2,0:T(8,128)S(1)} fusion(f32[2,512,1024]{1,2,0:T(8,128)S(1)} %get-tuple-element.5), kind=kOutput, calls=%fused_computation.38 | convolution fusion | flops 6446120960 | bytes 8388608 | tf_op jit(solution)/shard_map/kj,sjc->skc/dot_general | solution.py:14
  278.7 11.1 %fusion.17 = f32[2,1024,512]{1,2,0:T(8,128)S(1)} fusion(f32[2,512,1024]{1,2,0:T(8,128)S(1)} %get-tuple-element.6), kind=kOutput, calls=%fused_computation.36 | convolution fusion | flops 6446120960 | bytes 8388608 | tf_op jit(solution)/shard_map/kj,sjc->skc/dot_general | solution.py:14
  289.8 11.2 %convolution_subtract_fusion = f32[2,1024,512]{1,2,0:T(8,128)S(1)} fusion(f32[2,1024,512]{1,2,0:T(8,128)S(1)} %fusion.19, f32[2,512,1024]{1,2,0:T(8,128)S(1)} %get-tuple-element.6), kind=kOutput, calls=%fused_computation.18 | convolution fusion | flops 6447169536 | bytes 12582912 | tf_op jit(solution)/shard_map/kj,sjc->skc/dot_general | solution.py:14
  301.0 12.2 %multiply_subtract_fusion = (f32[2,1024,512]{1,2,0:T(8,128)S(1)}, f32[2,1024,512]{1,2,0:T(8,128)S(1)}) fusion(f32[2,1024,512]{1,2,0:T(8,128)S(1)} %convolution_subtract_fusion, f32[2,512]{1,0:T(2,128)S(1)} %get-tuple-element.20, f32[2,512]{1,0:T(2,128)S(1)} %get-tuple-element.19, f32[2,1024,512]{1,2,0:T(8,128)S(1)} %fusion.17, ...), kind=kOutput, calls=%fused_computation.13 | convolution fusion | flops 6453460992 | bytes 20979712 | tf_op jit(solution)/shard_map/kj,sjc->skc/dot_general | solution.py:14
  316.6 123.0 %all_to_all.40 = f32[2,2,32,16,1024]{4,3,1,0,2:T(8,128)S(1)} all-to-all(f32[2,2,32,16,1024]{4,3,1,0,2:T(8,128)S(1)} %copy.84), channel_id=1, replica_groups=mesh['ctx'=32,'fsdp'=4] {'ctx'}, dimensions={2} | all-to-all | bytes 16777216 | tf_op jit(solution)/shard_map/all_to_all | solution.py:86
  441.2 4.6 fusion
  445.9 4.7 subtract_bitcast_fusion.1
  451.8 31.8 %all_to_all.41 = f32[1,32,16,1024]{3,2,0,1:T(8,128)S(1)} all-to-all(f32[1,32,16,1024]{3,2,0,1:T(8,128)S(1)} %copy.75), channel_id=1, replica_groups=mesh['ctx'=32,'fsdp'=4] {'ctx'}, dimensions={1} | all-to-all | bytes 4194304 | tf_op jit(solution)/shard_map/all_to_all | solution.py:91
  483.7 2.9 fusion.7
  (32 shorter events, 18.1 us)
Async XLA Ops:
  6.5 1.2 copy-start.1
  6.5 1.5 copy-start.2
  6.5 217.4 %all-gather.2.cloned.1.call-start = ((), (), s32[]{:S(2)}) async-start(), calls=%async_computation.4 | async-start | bytes 20971520 | tf_op jit(solution)/shard_map/all_gather | solution.py:32
  9.4 26.5 %all-to-all-start = ((bf16[1,32,16,1024]{3,2,0,1:T(8,128)(2,1)}), bf16[1,32,16,1024]{3,2,0,1:T(8,128)(2,1)S(1)}, u32[]{:S(2)}, u32[]{:S(2)}) async-start(bf16[1,32,16,1024]{3,2,0,1:T(8,128)(2,1)} %bitcast.3), calls=%async_computation | async-start | bytes 2097152 | tf_op jit(solution)/shard_map/all_to_all | solution.py:48
  52.1 109.1 %all-to-all-start.1 = ((f32[2,64,16,1024]{3,2,0,1:T(8,128)}), f32[2,64,16,1024]{3,2,0,1:T(8,128)}, u32[]{:S(2)}, u32[]{:S(2)}) async-start(f32[2,64,16,1024]{3,2,0,1:T(8,128)} %copy.55), calls=%async_computation.1 | async-start | bytes 16777216 | tf_op jit(solution)/shard_map/all_to_all | solution.py:60
  167.7 2.0 copy-start
  450.6 33.1 %copy-start.3 = (bf16[512,1024]{1,0:T(8,128)(2,1)S(1)}, bf16[512,1024]{1,0:T(8,128)(2,1)}, u32[]{:S(2)}) copy-start(bf16[512,1024]{1,0:T(8,128)(2,1)} %param.7) | copy-start | bytes 3145732
  450.6 33.1 %copy-start.4 = (f32[1024]{0:T(1024)S(1)}, f32[1024]{0:T(1024)}, u32[]{:S(2)}) copy-start(f32[1024]{0:T(1024)} %param.8) | copy-start | bytes 12292
Sparse Core Ops, SparseCore 0:
  9.0 157.0 all-gather.1
where the time goes:
time: 503 us; the launch traced here: 494 us
  blocking collectives  155 us (31%)
  matrix products  141 us (28%)
  waiting for transfers between devices  121 us (24%)
  local copies, waits for them, and re-layouts  37.1 us (7%)
  starting transfers between devices  14.4 us (3%)
  between operations  13.8 us (3%)
  other arithmetic  11.1 us (2%)
    dot_general x8, matrix products, contract(): jnp.einsum('kj,sjc->skc', matrix, operand, precision=lax.Precision.HIGHEST)  125 us
    all_to_all x1, blocking collectives, body(): lax.all_to_all(stacked, 'ctx', split_axis=2, concat_axis=1, tiled=True)  123 us
    all_to_all x1, waiting for transfers between devices, body(): lax.all_to_all(spread, 'ctx', split_axis=1, concat_axis=2, tiled=True)  104 us
    all_to_all x1, blocking collectives, body(): lax.all_to_all(folded, 'ctx', split_axis=1, concat_axis=1, tiled=True)  31.8 us
    all_to_all x1, waiting for transfers between devices, body(): lax.all_to_all(source.reshape(source.shape[0], devices, block_rows, width...  16.5 us
    dot_general x4, matrix products, mix_rows(): jnp.einsum('kp,pjc->kjc', matrix, operand, precision=lax.Precision.HIGHEST)  15.6 us
    squeeze x2, local copies, waits for them, and re-layouts, body(): prod_real = freq_real * filter_float[0] - freq_imag * filter_float[1]  10.8 us
  transfers between devices with their start and end apart: 3, of which 2 were waited for; matrix products, arithmetic and copies ran while one was open for 16% of the time, Pallas kernels for 0%

commit v1 on v0

--- a/solution.py
+++ b/solution.py
@@ -3,6 +3,18 @@
 import jax.numpy as jnp
 from jax import lax
 from jax.sharding import PartitionSpec as P
+
+
+def draft_the_task(state, axis_k, array_axis):
+    return jnp.concatenate(
+        lax.all_to_all(
+            jnp.stack(jnp.split(state, lax.axis_size("ctx"), axis=axis_k)),
+            axis_name="ctx",
+            concat_axis=0,
+            split_axis=0,
+        ),
+        axis=array_axis,
+    )
 
 
 def phase_angles(rows_side, cols_side, modulus):
@@ -45,13 +57,9 @@
     twist_sin = jnp.sin(twist_angle)[:, :, None]
     source = mixed[None]
     width_now = source.shape[2]
-    real_in = lax.all_to_all(
-        source.reshape(source.shape[0], devices, block_rows, width_now),
-        "ctx",
-        split_axis=1,
-        concat_axis=1,
-        tiled=True,
-    )[0].astype(jnp.float32)
+    real_in = draft_the_task(source.reshape(source.shape[0], devices, block_rows, width_now), 1, 1)[
+        0
+    ].astype(jnp.float32)
     real_mix = mix_rows(cross_cos, real_in)
     imag_mix = -mix_rows(cross_sin, real_in)
     spread = jnp.stack(

time: 503 us -> 576 us (1.15)
  local copies, waits for them, and re-layouts: 37.1 us -> 109 us
    unnamed x10 -> x41, local copies, waits for them, and re-layouts: 2.27 us -> 19.6 us
    squeeze x0 -> x2, local copies, waits for them, and re-layouts: none -> 12.3 us  [the longest x1 6.22 us: body(): imag_block = received[1, :, 0]]
    slice x2, local copies, waits for them, and re-layouts: 2.18 us -> 13.7 us  [body(): real_part = regrouped[0]]
    all_to_all x1, local copies, waits for them, and re-layouts: 4.23 us -> 15.4 us  [body(): lax.all_to_all(spread, 'ctx', split_axis=1, concat_axis=2, tiled=True)]
    slice x0 -> x2, local copies, waits for them, and re-layouts: none -> 8.42 us  [body(): imag_block = received[1, :, 0]]
  transfers between devices with their start and end apart: 3 -> 3, of which waited for: 2 -> 2; matrix products, arithmetic and copies ran while one was open for 16% -> 22% of each run, Pallas kernels for 0% -> 0%
where the time goes in v1:
time: 576 us; the launch traced here: 566 us
  blocking collectives  155 us (27%)
  matrix products  142 us (25%)
  waiting for transfers between devices  121 us (21%)
  local copies, waits for them, and re-layouts  109 us (19%)
  starting transfers between devices  14.3 us (2%)
  between operations  13.8 us (2%)
  other arithmetic  10.1 us (2%)
    dot_general x8, matrix products, contract(): jnp.einsum('kj,sjc->skc', matrix, operand, precision=lax.Precision.HIGHEST)  125 us
    all_to_all x1, blocking collectives, body(): lax.all_to_all(stacked, 'ctx', split_axis=2, concat_axis=1, tiled=True)  123 us
    all_to_all x1, waiting for transfers between devices, body(): lax.all_to_all(spread, 'ctx', split_axis=1, concat_axis=2, tiled=True)  104 us
    all_to_all x1, blocking collectives, body(): lax.all_to_all(folded, 'ctx', split_axis=1, concat_axis=1, tiled=True)  31.8 us
    unnamed x41, local copies, waits for them, and re-layouts  19.6 us
    dot_general x4, matrix products, mix_rows(): jnp.einsum('kp,pjc->kjc', matrix, operand, precision=lax.Precision.HIGHEST)  17.3 us
    all_to_all x1, waiting for transfers between devices, draft_the_task(): lax.all_to_all(jnp.stack(jnp.split(state, lax.axis_size('ctx'), axis=axis...  16.5 us
    all_to_all x1, local copies, waits for them, and re-layouts, body(): lax.all_to_all(spread, 'ctx', split_axis=1, concat_axis=2, tiled=True)  15.4 us
  transfers between devices with their start and end apart: 3, of which 2 were waited for; matrix products, arithmetic and copies ran while one was open for 22% of the time, Pallas kernels for 0%

profile of v1, /device:TPU:1, one launch (start us, length us, event | category | flops | bytes accessed | tf_op | source)
XLA Modules:
  0.0 565.8 jit_solution(1783539589394685823)
XLA Ops:
  29.1 9.6 %all-to-all-start = ((bf16[32,1,1,16,1024]{4,3,2,1,0:T(8,128)(2,1)}), bf16[32,1,1,16,1024]{4,3,2,1,0:T(8,128)(2,1)S(1)}, u32[]{:S(2)}, u32[]{:S(2)}) async-start(bf16[32,1,1,16,1024]{4,3,2,1,0:T(8,128)(2,1)} %constant_dynamic-update-slice_fusion), calls=%async_computation | async-start | bytes 2097152 | tf_op jit(solution)/shard_map/all_to_all | solution.py:10
  39.1 16.5 %all-to-all-done = bf16[32,1,1,16,1024]{4,3,2,1,0:T(8,128)(2,1)S(1)} async-done(((bf16[32,1,1,16,1024]{4,3,2,1,0:T(8,128)(2,1)}), bf16[32,1,1,16,1024]{4,3,2,1,0:T(8,128)(2,1)S(1)}, u32[]{:S(2)}, u32[]{:S(2)}) %all-to-all-start) | async-done | bytes 1048608 | tf_op jit(solution)/shard_map/all_to_all | solution.py:10
  63.6 8.6 %copy.1475 = f32[2,64,16,1024]{3,2,0,1:T(8,128)} copy(f32[2,64,16,1024]{3,1,2,0:T(8,128)S(1)} %pad_maximum_fusion) | data formatting | bytes 16777216 | tf_op jit(solution)/shard_map/stack | solution.py:65
  77.1 104.1 %all-to-all-done.1 = f32[2,64,16,1024]{3,2,0,1:T(8,128)} async-done(((f32[2,64,16,1024]{3,2,0,1:T(8,128)}), f32[2,64,16,1024]{3,2,0,1:T(8,128)}, u32[]{:S(2)}, u32[]{:S(2)}) %all-to-all-start.1) | async-done | bytes 8388640 | tf_op jit(solution)/shard_map/all_to_all | solution.py:68
  181.2 15.4 %copy.1517 = f32[2,32,2,16,1024]{4,2,1,3,0:T(2,128)} copy(f32[2,32,2,16,1024]{4,3,0,2,1:T(8,128)} %bitcast.39) | data formatting | bytes 16777216 | tf_op jit(solution)/shard_map/all_to_all | solution.py:68
  196.6 9.1 %fusion.129 = (f32[1,2,32,16,1024]{4,1,2,3,0:T(2,128)}, f32[1,2,32,16,1024]{4,1,2,3,0:T(2,128)S(1)}) fusion(f32[2,2,32,16,1024]{4,1,2,3,0:T(2,128)} %bitcast.237), kind=kLoop, calls=%fused_computation.223 | loop fusion | bytes 16777216 | tf_op jit(solution)/shard_map/slice | solution.py:73
  212.8 17.2 %fusion.17 = f32[2,1024,512]{2,1,0:T(8,128)S(1)} fusion(f32[2,512,1024]{2,1,0:T(8,128)S(1)} %bitcast.235), kind=kOutput, calls=%fused_computation.40 | convolution fusion | flops 6446120960 | bytes 8388608 | tf_op jit(solution)/shard_map/kj,sjc->skc/dot_general | solution.py:26
  230.0 18.3 %fusion.15 = f32[2,1024,512]{2,1,0:T(8,128)} fusion(f32[2,512,1024]{2,1,0:T(8,128)S(1)} %bitcast.233), kind=kOutput, calls=%fused_computation.38 | convolution fusion | flops 6446120960 | bytes 8388608 | tf_op jit(solution)/shard_map/kj,sjc->skc/dot_general | solution.py:26
  248.3 18.8 %convolution_add_fusion.1 = f32[2,1024,512]{2,1,0:T(8,128)} fusion(f32[2,1024,512]{2,1,0:T(8,128)S(1)} %fusion.17, f32[2,512,1024]{2,1,0:T(8,128)S(1)} %bitcast.234), kind=kOutput, calls=%fused_computation.18 | convolution fusion | flops 6447169536 | bytes 12582912 | tf_op jit(solution)/shard_map/kj,sjc->skc/dot_general | solution.py:26
  274.4 5.4 copy.1484
  279.8 5.4 copy.1481
  285.2 25.7 %fusion = (f32[2,512,1024]{1,2,0:T(8,128)S(1)}, f32[2,512,1024]{1,2,0:T(8,128)S(1)}) fusion(f32[2,512,1024]{1,2,0:T(8,128)} %copy.1484, f32[2,512,1024]{1,2,0:T(8,128)} %copy.1481, f32[2,1024,512]{2,1,0:T(8,128)} %convolution_add_fusion.1, f32[2,1024,512]{2,1,0:T(8,128)} %fusion.15, f32[2,512,1024]{2,1,0:T(8,128)} %bitcast.236), kind=kOutput, calls=%fused_computation.6 | convolution fusion | flops 6453460992 | bytes 29360128 | tf_op jit(solution)/shard_map/kj,sjc->skc/dot_general | solution.py:26
  311.0 10.7 %fusion.13 = f32[2,1024,512]{1,2,0:T(8,128)S(1)} fusion(f32[2,512,1024]{1,2,0:T(8,128)S(1)} %get-tuple-element.5), kind=kOutput, calls=%fused_computation.36 | convolution fusion | flops 6446120960 | bytes 8388608 | tf_op jit(solution)/shard_map/kj,sjc->skc/dot_general | solution.py:26
  321.6 11.3 %fusion.11 = f32[2,1024,512]{1,2,0:T(8,128)S(1)} fusion(f32[2,512,1024]{1,2,0:T(8,128)S(1)} %get-tuple-element.6), kind=kOutput, calls=%fused_computation.34 | convolution fusion | flops 6446120960 | bytes 8388608 | tf_op jit(solution)/shard_map/kj,sjc->skc/dot_general | solution.py:26
  333.0 11.2 %convolution_subtract_fusion = f32[2,1024,512]{1,2,0:T(8,128)S(1)} fusion(f32[2,1024,512]{1,2,0:T(8,128)S(1)} %fusion.13, f32[2,512,1024]{1,2,0:T(8,128)S(1)} %get-tuple-element.6), kind=kOutput, calls=%fused_computation.16 | convolution fusion | flops 6447169536 | bytes 12582912 | tf_op jit(solution)/shard_map/kj,sjc->skc/dot_general | solution.py:26
  344.2 12.0 %multiply_subtract_fusion = (f32[2,1024,512]{1,2,0:T(8,128)S(1)}, f32[2,1024,512]{1,2,0:T(8,128)S(1)}) fusion(f32[2,1024,512]{1,2,0:T(8,128)S(1)} %convolution_subtract_fusion, f32[2,512]{1,0:T(2,128)S(1)} %get-tuple-element.20, f32[2,512]{1,0:T(2,128)S(1)} %get-tuple-element.19, f32[2,1024,512]{1,2,0:T(8,128)S(1)} %fusion.11, ...), kind=kOutput, calls=%fused_computation.11 | convolution fusion | flops 6453460992 | bytes 20979712 | tf_op jit(solution)/shard_map/kj,sjc->skc/dot_general | solution.py:26
  359.5 123.4 %all_to_all.40 = f32[2,2,32,16,1024]{4,3,1,0,2:T(8,128)} all-to-all(f32[2,2,32,16,1024]{4,3,1,0,2:T(8,128)S(1)} %copy.1491), channel_id=1, replica_groups=mesh['ctx'=32,'fsdp'=4] {'ctx'}, dimensions={2} | all-to-all | bytes 16777216 | tf_op jit(solution)/shard_map/all_to_all | solution.py:94
  490.3 5.2 copy.1493
  495.5 6.1 %squeeze.24 = f32[64,16,1024]{2,0,1:T(8,128)} reshape(f32[1,32,2,1,16,1024]{5,2,1,4,3,0:T(2,128)} %copy.1493) | data formatting | bytes 8388608 | tf_op jit(solution)/shard_map/squeeze | solution.py:95
  501.6 5.9 %fusion.47 = f32[32,16,1024]{2,0,1:T(8,128)} fusion(f32[64,16,1024]{2,0,1:T(8,128)} %squeeze.24, s32[64]{0:T(128)S(1)} %mul.274), kind=kOutput, calls=%fused_computation.132 | convolution fusion | flops 402683904 | bytes 6291712 | tf_op jit(solution)/shard_map/kp,pjc->kjc/dot_general | solution.py:30
  507.5 5.2 copy.1494
  512.7 6.2 %squeeze.25 = f32[64,16,1024]{2,0,1:T(8,128)} reshape(f32[1,32,2,1,16,1024]{5,2,1,4,3,0:T(2,128)} %copy.1494) | data formatting | bytes 8388608 | tf_op jit(solution)/shard_map/squeeze | solution.py:96
  518.9 5.1 subtract_bitcast_fusion.1
  525.3 31.8 %all_to_all.41 = f32[1,32,16,1024]{3,2,0,1:T(8,128)S(1)} all-to-all(f32[1,32,16,1024]{3,2,0,1:T(8,128)S(1)} %copy.1495), channel_id=1, replica_groups=mesh['ctx'=32,'fsdp'=4] {'ctx'}, dimensions={1} | all-to-all | bytes 4194304 | tf_op jit(solution)/shard_map/all_to_all | solution.py:99
  (69 shorter events, 63.7 us)
Async XLA Ops:
  6.5 1.2 copy-start.2
  6.5 260.6 %all-gather.2.cloned.1.call-start = ((), (), s32[]{:S(2)}) async-start(), calls=%async_computation.4 | async-start | bytes 20971520 | tf_op jit(solution)/shard_map/all_gather | solution.py:44
  29.1 26.5 %all-to-all-start = ((bf16[32,1,1,16,1024]{4,3,2,1,0:T(8,128)(2,1)}), bf16[32,1,1,16,1024]{4,3,2,1,0:T(8,128)(2,1)S(1)}, u32[]{:S(2)}, u32[]{:S(2)}) async-start(bf16[32,1,1,16,1024]{4,3,2,1,0:T(8,128)(2,1)} %constant_dynamic-update-slice_fusion), calls=%async_computation | async-start | bytes 2097152 | tf_op jit(solution)/shard_map/all_to_all | solution.py:10
  72.1 109.1 %all-to-all-start.1 = ((f32[2,64,16,1024]{3,2,0,1:T(8,128)}), f32[2,64,16,1024]{3,2,0,1:T(8,128)}, u32[]{:S(2)}, u32[]{:S(2)}) async-start(f32[2,64,16,1024]{3,2,0,1:T(8,128)} %copy.1475), calls=%async_computation.1 | async-start | bytes 16777216 | tf_op jit(solution)/shard_map/all_to_all | solution.py:68
  210.4 2.4 copy-start
  501.6 5.9 %copy-start.1 = (f32[1,32,2,1,16,1024]{5,4,1,2,0,3:T(8,128)S(1)}, f32[1,32,2,1,16,1024]{5,4,1,2,0,3:T(8,128)}, u32[]{:S(2)}) copy-start(f32[1,32,2,1,16,1024]{5,4,1,2,0,3:T(8,128)} %get-tuple-element.11) | copy-start | bytes 12582916
  524.1 33.1 %copy-start.3 = (bf16[512,1024]{1,0:T(8,128)(2,1)S(1)}, bf16[512,1024]{1,0:T(8,128)(2,1)}, u32[]{:S(2)}) copy-start(bf16[512,1024]{1,0:T(8,128)(2,1)} %param.7) | copy-start | bytes 3145732
  524.1 33.1 %copy-start.4 = (f32[1024]{0:T(1024)S(1)}, f32[1024]{0:T(1024)}, u32[]{:S(2)}) copy-start(f32[1024]{0:T(1024)} %param.8) | copy-start | bytes 12292
Sparse Core Ops, SparseCore 0:
  9.0 157.0 all-gather.1
